TPU v7x, 128 devices: a whole 4x4x4 slice. The times are simulated.
128 devices in a mesh: rows: 32 (over x, y, core), cols: 4 (over z).
Axes of the slice: x: 4, y: 4, z: 4, core: 2. Of those that a mesh axis runs over, the one named last changes fastest.
Arguments:
- history_owner: int32 [128, 1024, 1], P('rows'), may hold values from 0 to 31; in each aligned block of 1024 rows (0 to 1023, 1024 to 2047, ..., all dimensions but the last counted through in order) at most 48 rows name the same one
- history_row: int32 [128, 1024], P('rows'), may hold values from 0 to 4095
- candidate_owner: int32 [128, 512, 1], P('rows'), may hold values from 0 to 31; in each aligned block of 512 rows (0 to 511, 512 to 1023, ..., all dimensions but the last counted through in order) at most 24 rows name the same one
- candidate_row: int32 [128, 512], P('rows'), may hold values from 0 to 4095
- history_length: int32 [128], P('rows'), may hold values from 256 to 1024, as said below
- embed_table: bfloat16 [131072, 1024], P('rows', 'cols'), may hold values from -7 to 7
- query_weight: bfloat16 [2, 1024, 1024], replicated, may hold values from -9 to 9
- output_weight: bfloat16 [2, 1024, 1024], replicated, may hold values from -0.1875 to 0.1875
- score_weight: float32 [1024], replicated, may hold values from -0.1875 to 0.1875
- logit_grad: float32 [128, 512], P(('rows', 'cols')), may hold values from -192 to 192
Outputs:
- logits: float32 [128, 512], P(('rows', 'cols'))
- table_grad: float32 [131072, 1024], P('rows', 'cols')
Inputs may be any that keep to these rules, and one draw needn't show every extreme that they name: `history_owner`: within one user's history no owner index is named more than 48 times. `candidate_owner`: within one user's candidates no owner index is named more than 24 times. `history_length`: some user's length is 1024.
All inputs are finite; a program needn't handle non-finite values.
Results may differ from a plain program's by a relative error of at most 0.033.
The roundings to bfloat16 on the way count: a program that leaves them out, or rounds other values in their place, can miss the bound.
Values may be sent and summed in bfloat16 or wider, within the bound.
No kernel may reach another device: no remote copies, remote signals or barrier semaphores. Data moves between devices by JAX's collectives and lax.ppermute only.
A program may use at most 192 MiB of HBM per device.

v0:
```python
import functools
import math

import jax
import jax.numpy as jnp
from jax import lax
from jax.experimental import pallas as pl
from jax.experimental.pallas import tpu as pltpu
from jax.sharding import PartitionSpec as P

HEADS = 8
BF = jnp.bfloat16
F32 = jnp.float32
NN = (((1,), (0,)), ((), ()))
NT = (((1,), (1,)), ((), ()))
TN = (((0,), (0,)), ((), ()))
VMEM_SPEC = pl.BlockSpec(memory_space=pltpu.VMEM)
SMEM_SPEC = pl.BlockSpec(memory_space=pltpu.SMEM)
MIB = 1024 * 1024


def dot(a, b, dims):
    return lax.dot_general(a, b, dims, preferred_element_type=F32)


def iota(shape, axis):
    return lax.broadcasted_iota(jnp.int32, shape, axis)


def request_kernel(me, h_own, h_row, c_own, c_row, req, h_pos, c_pos, *, rows, most_h, most_c):
    users, hist = h_own.shape
    cand = c_own.shape[1]
    before = (iota((hist, hist), 0) < iota((hist, hist), 1)).astype(BF)
    for u in range(users):
        parts = []
        for own, row, base, most, pos in (
            (h_own, h_row, 0, most_h, h_pos),
            (c_own, c_row, most_h, most_c, c_pos),
        ):
            n = own.shape[1]
            owner = own[u : u + 1, :]
            match = (iota((rows, n), 0) == owner).astype(F32)
            earlier = dot(match.astype(BF), before[:n, :n], NN)
            rank = jnp.sum(match * earlier, axis=0, keepdims=True).astype(jnp.int32)

            @pl.when(me[0] == u)
            def _():
                pos[...] = owner * 48 + rank

            ids = row[u : u + 1, :]
            high = (match * (ids >> 6).astype(F32)).astype(BF)
            low = (match * (ids & 63).astype(F32)).astype(BF)
            hit = (iota((128, n), 0) == rank + base).astype(BF)
            parts.append(dot(jnp.concatenate([high, low], axis=0), hit, NT))
        both = parts[0] + parts[1]
        req[:, u, :] = (both[:rows] * 64.0 + both[rows:]).astype(jnp.int32)


def gather_kernel(idx, table, out, wide, stage, *, first, count):
    n_rows = table.shape[0]
    chunk = 256

    def widen(i, carry):
        at = pl.multiple_of(i * chunk, chunk)
        block = table[pl.ds(at, chunk), :].astype(F32)
        wide[pl.ds(at, chunk), 0, :] = block[:, :128]
        wide[pl.ds(at, chunk), 1, :] = block[:, 128:]
        return carry

    lax.fori_loop(0, n_rows // chunk, widen, 0)

    def fetch(u, carry):
        for s in range(count):
            stage[s] = wide[idx[u, first + s]]
        out[u] = jnp.concatenate([stage[:, 0, :], stage[:, 1, :]], axis=0).astype(BF)
        return carry

    lax.fori_loop(0, out.shape[0], fetch, 0)


def add_rows(idx, grads, stage, sums, first, count):
    def add(u, carry):
        block = grads[u].astype(F32)
        stage[:, 0, :] = block[:count]
        stage[:, 1, :] = block[count:]
        for s in range(count):
            total = sums[s % len(sums)]
            at = idx[u, first + s]
            total[at] = total[at] + stage[s]
        return carry

    lax.fori_loop(0, grads.shape[0], add, 0)


def scatter_first_kernel(idx, grads, out, stage, other, *, first, count):
    out[...] = jnp.zeros_like(out)
    other[...] = jnp.zeros_like(other)
    add_rows(idx, grads, stage, (out, other), first, count)
    chunk = 128

    def finish(i, carry):
        at = pl.ds(pl.multiple_of(i * chunk, chunk), chunk)
        out[at] = out[at] + other[at]
        return carry

    lax.fori_loop(0, out.shape[0] // chunk, finish, 0)


def scatter_last_kernel(idx, grads, start, out, stage, pair, *, first, count):
    add_rows(idx, grads, stage, (start,), first, count)
    chunk = pair.shape[0]

    def finish(i, carry):
        at = pl.ds(pl.multiple_of(i * chunk, chunk), chunk)
        pair[...] = start[at]
        out[at, 0:128] = pair[:, 0, :]
        out[at, 128:256] = pair[:, 1, :]
        return carry

    lax.fori_loop(0, out.shape[0] // chunk, finish, 0)


def prepare_kernel(recv, h_pos, c_pos, wq, pt_h, pt_c, cand, q1, wq0, sems):
    load = pltpu.make_async_copy(wq.at[0], wq0, sems.at[0])
    load.start()
    slots, hist = pt_h.shape
    n_cand = cand.shape[0]
    cols = recv.shape[1]
    for at in range(0, slots, 256):
        place = iota((256, n_cand), 0) + at
        pt_c[at : at + 256, 0:n_cand] = jnp.where(place == c_pos[...], 1.0, 0.0).astype(BF)
        pt_c[at : at + 256, n_cand:] = jnp.where(place == c_pos[...] + 24, 1.0, 0.0).astype(BF)
    for c in range(0, cols, 2):
        both = jnp.concatenate([recv[:, c].reshape(slots, 128), recv[:, c + 1].reshape(slots, 128)], axis=1)
        got = dot(pt_c[...], both, TN).astype(BF)
        for k in range(2):
            at = (c + k) * 256
            cand[:, at : at + 128] = got[:n_cand, k * 128 : k * 128 + 128]
            cand[:, at + 128 : at + 256] = got[n_cand:, k * 128 : k * 128 + 128]
    load.wait()
    q1[...] = dot(cand[...], wq0[...], NN).astype(BF)
    for at in range(0, slots, 256):
        place = iota((256, hist), 0) + at
        pt_h[at : at + 256, :] = jnp.where(place == h_pos[...], 1.0, 0.0).astype(BF)


def user_kernel(
    length, recv_in, pt_in, cand_in, q1_in, wq_in, wo_in, lg_row, sw, u_row,
    send_out, d_q_out, d_stream_out, logits,
    recv, pt_h, cand, q1, wq1, wo0, keys, q2, att1, soft, d_keys, d_q, d_att, d_stream, in_sems, out_sems,
):
    hist = keys.shape[0]
    n_cand = cand.shape[0]
    cols = recv_in.shape[1]
    rows = recv_in.shape[0]
    slots = pt_h.shape[0]
    inv_root = 1.0 / math.sqrt(128)
    pairs = [(pt_in, pt_h)] + [(recv_in.at[:, c], recv.at[c]) for c in range(cols)]
    pairs += [(q1_in, q1), (cand_in, cand), (wo_in.at[0], wo0), (wq_in.at[1], wq1)]
    loads = [pltpu.make_async_copy(src, dst, in_sems.at[i]) for i, (src, dst) in enumerate(pairs)]
    for load in loads:
        load.start()
    loads[0].wait()
    for c in range(cols):
        loads[1 + c].wait()
        both = jnp.concatenate(
            [recv[c, :, 0:48, :].reshape(slots, 128), recv[c, :, 48:96, :].reshape(slots, 128)], axis=1
        )
        keys[:, c * 256 : c * 256 + 256] = dot(pt_h[...], both, TN).astype(BF)
    for load in loads[1 + cols :]:
        load.wait()

    lg = jnp.transpose(jnp.broadcast_to(lg_row[...], (8, n_cand)))[:, 0:1]
    bias = jnp.where(iota((1, hist), 1) < length[0], 0.0, -1e30)
    scale = inv_root * math.log2(math.e)

    def softmax(q, k):
        scores = dot(q, k, NT) + bias
        top = jnp.max(scores, axis=1, keepdims=True)
        e = jnp.exp2((scores - top) * scale)
        return e * (1.0 / jnp.sum(e, axis=1, keepdims=True))

    def first_layer(h, carry):
        hs = pl.ds(pl.multiple_of(h * 128, 128), 128)
        k = keys[:, hs]
        y = softmax(q1[:, hs], k)
        soft[h] = y
        att1[:, hs] = dot(y.astype(BF), k, NN).astype(BF)
        return carry

    lax.fori_loop(0, HEADS, first_layer, 0)
    stream = cand[...].astype(F32) + dot(att1[...], wo0[...], NN)
    q2[...] = dot(stream.astype(BF), wq1[...], NN).astype(BF)
    score = jnp.sum(stream * sw[...], axis=1, keepdims=True)
    lgs = lg * inv_root

    def second_layer(h, score):
        hs = pl.ds(pl.multiple_of(h * 128, 128), 128)
        k = keys[:, hs]
        q = q2[:, hs]
        u = u_row[:, hs]
        y = softmax(q, k)
        w = y.astype(BF)
        attended = dot(w, k, NN).astype(BF).astype(F32)
        u_hi = u.astype(BF).astype(F32)
        u_mid = (u - u_hi).astype(BF).astype(F32)
        u_low = u - u_hi - u_mid
        line = iota((8, 128), 0)
        pieces = jnp.where(line == 0, u_hi, jnp.where(line == 1, u_mid, jnp.where(line == 2, u_low, 0.0)))
        g = jnp.sum(dot(pieces.astype(BF), k, NT), axis=0, keepdims=True)
        mean = jnp.sum(y * g, axis=1, keepdims=True)
        ds = (y * lgs * (g - mean)).astype(BF)
        d_q[:, hs] = dot(ds, k, NN).astype(BF)
        da = (lg * u).astype(BF)
        d_keys[:, hs] = dot(ds, q, TN) + dot(w, da, TN)
        return score + jnp.sum(attended * u, axis=1, keepdims=True)

    score = lax.fori_loop(0, HEADS, second_layer, score)
    logits[...] = score
    d_after = lg * sw[...] + dot(d_q[...], wq1[...], NT).astype(BF).astype(F32)
    d_stream[...] = d_after
    d_att[...] = dot(d_after.astype(BF), wo0[...], NT).astype(BF)
    put_stream = pltpu.make_async_copy(d_stream, d_stream_out, out_sems.at[0])
    put_stream.start()

    def first_back(h, carry):
        hs = pl.ds(pl.multiple_of(h * 128, 128), 128)
        k = keys[:, hs]
        y = soft[h]
        da = d_att[:, hs]
        dw = dot(da, k, NT)
        mean = jnp.sum(y * dw, axis=1, keepdims=True)
        ds = (y * (dw - mean)).astype(BF)
        d_q[:, hs] = (dot(ds, k, NN) * inv_root).astype(BF)
        grad = d_keys[:, hs] + dot(ds, q1[:, hs], TN) * inv_root + dot(y.astype(BF), da, TN)
        keys[:, hs] = grad.astype(BF)
        return carry

    lax.fori_loop(0, HEADS, first_back, 0)
    puts = [put_stream, pltpu.make_async_copy(d_q, d_q_out, out_sems.at[1])]
    puts[1].start()
    for c in range(cols):
        got = dot(pt_h[...], keys[:, c * 256 : c * 256 + 256], NN).astype(BF)
        recv[c, :, 0:48, :] = got[:, :128].reshape(rows, 48, 128)
        recv[c, :, 48:96, :] = got[:, 128:].reshape(rows, 48, 128)
        put = pltpu.make_async_copy(recv.at[c], send_out.at[:, c], out_sems.at[2 + c])
        put.start()
        puts.append(put)
    for put in puts:
        put.wait()


def finish_kernel(d_q, d_stream, pt_c, wq_in, send, wq0, grad, sem):
    load = pltpu.make_async_copy(wq_in.at[0], wq0, sem.at[0])
    load.start()
    load.wait()
    rows, cols = send.shape[0], send.shape[1]
    grad[...] = (d_stream[...] + dot(d_q[...], wq0[...], NT).astype(BF).astype(F32)).astype(BF)
    for c in range(0, cols, 2):
        at = c * 256
        even = jnp.concatenate([grad[:, at : at + 128], grad[:, at + 256 : at + 384]], axis=1)
        odd = jnp.concatenate([grad[:, at + 128 : at + 256], grad[:, at + 384 : at + 512]], axis=1)
        got = dot(pt_c[...], jnp.concatenate([even, odd], axis=0), NN).astype(BF)
        send[:, c] = got[:, :128].reshape(rows, 48, 128)
        send[:, c + 1] = got[:, 128:].reshape(rows, 48, 128)


def call(kernel, name, mib, out_shape, in_specs, out_specs, scratch=(), **static):
    return pl.pallas_call(
        functools.partial(kernel, **static),
        out_shape=out_shape,
        in_specs=in_specs,
        out_specs=out_specs,
        scratch_shapes=list(scratch),
        compiler_params=pltpu.CompilerParams(vmem_limit_bytes=mib * MIB),
        name=name,
    )


def shape(dims, kind):
    return jax.ShapeDtypeStruct(dims, kind)


def body(
    history_owner, history_row, candidate_owner, candidate_row, history_length,
    embed_table, query_weight, output_weight, score_weight, logit_grad,
):
    n_rows = lax.axis_size("rows")
    n_cols = lax.axis_size("cols")
    users, hist = history_row.shape
    cand = candidate_row.shape[1]
    most_h = 3 * hist // (2 * n_rows)
    most_c = 3 * cand // (2 * n_rows)
    table_rows, col_width = embed_table.shape
    width = n_cols * col_width
    peers = n_rows * n_cols
    slots = n_rows * most_h
    me = lax.axis_index("cols").astype(jnp.int32)
    V, S, A = VMEM_SPEC, SMEM_SPEC, pl.BlockSpec(memory_space=pl.ANY)
    req, h_pos, c_pos = call(
        request_kernel, "requests", 16,
        (shape((n_rows, users, 128), jnp.int32), shape((1, hist), jnp.int32), shape((1, cand), jnp.int32)),
        [S, V, V, V, V], (V, V, V), rows=n_rows, most_h=most_h, most_c=most_c,
    )(me.reshape(1), history_owner[:, :, 0], history_row, candidate_owner[:, :, 0], candidate_row)
    wanted = lax.all_to_all(req, "rows", split_axis=0, concat_axis=0, tiled=True)
    wanted = wanted.reshape(peers, 128)

    def gather(first, count):
        return call(
            gather_kernel, "gather_rows", 16, shape((peers, 2 * count, 128), BF), [S, V], V,
            [pltpu.VMEM((table_rows, 2, 128), F32), pltpu.VMEM((count, 2, 128), F32)],
            first=first, count=count,
        )

    def exchange(x, label):
        with jax.named_scope(label):
            return lax.all_to_all(x, ("rows", "cols"), split_axis=0, concat_axis=0, tiled=True)

    found_c = gather(most_h, most_c)(wanted, embed_table)
    back_c = exchange(found_c, "fetch_c")
    found_h = gather(0, most_h)(wanted, embed_table)
    back_h = exchange(found_h, "fetch_h")
    length = lax.dynamic_slice_in_dim(history_length, me, 1)
    with jax.named_scope("score_row"):
        u_row = jnp.dot(
            output_weight[1].astype(F32), score_weight, precision=lax.Precision.HIGHEST
        ).reshape(1, -1)
    pt_h, pt_c, cand_rows, q1 = call(
        prepare_kernel, "prepare", 24,
        (shape((slots, hist), BF), shape((slots, 2 * cand), BF), shape((cand, width), BF), shape((cand, width), BF)),
        [V, V, V, A], (V, V, V, V),
        [pltpu.VMEM((width, width), BF), pltpu.SemaphoreType.DMA((1,))],
    )(back_c.reshape(n_rows, n_cols, 2 * most_c, 128), h_pos, c_pos, query_weight)
    send_h, d_q, d_stream, logits = call(
        user_kernel, "user_pass", 52,
        (
            shape((n_rows, n_cols, 2 * most_h, 128), BF), shape((cand, width), BF),
            shape((cand, width), F32), shape((cand, 1), F32),
        ),
        [S, A, A, A, A, A, A, V, V, V], (A, A, A, V),
        [
            pltpu.VMEM((n_cols, n_rows, 2 * most_h, 128), BF),
            pltpu.VMEM((slots, hist), BF),
            pltpu.VMEM((cand, width), BF),
            pltpu.VMEM((cand, width), BF),
            pltpu.VMEM((width, width), BF),
            pltpu.VMEM((width, width), BF),
            pltpu.VMEM((hist, width), BF),
            pltpu.VMEM((cand, width), BF),
            pltpu.VMEM((cand, width), BF),
            pltpu.VMEM((HEADS, cand, hist), F32),
            pltpu.VMEM((hist, width), F32),
            pltpu.VMEM((cand, width), BF),
            pltpu.VMEM((cand, width), BF),
            pltpu.VMEM((cand, width), F32),
            pltpu.SemaphoreType.DMA((5 + n_cols,)),
            pltpu.SemaphoreType.DMA((2 + n_cols,)),
        ],
    )(
        length, back_h.reshape(n_rows, n_cols, 2 * most_h, 128), pt_h, cand_rows, q1,
        query_weight, output_weight, logit_grad, score_weight.reshape(1, -1), u_row,
    )
    grads_h = exchange(send_h.reshape(peers, 2 * most_h, 128), "return_h")
    send_c = call(
        finish_kernel, "finish", 20, shape((n_rows, n_cols, 2 * most_c, 128), BF), [V, V, V, A], V,
        [pltpu.VMEM((width, width), BF), pltpu.VMEM((cand, width), BF), pltpu.SemaphoreType.DMA((1,))],
    )(d_q, d_stream, pt_c, query_weight)
    grads_c = exchange(send_c.reshape(peers, 2 * most_c, 128), "return_c")
    half = call(
        scatter_first_kernel, "scatter_history", 18, shape((table_rows, 2, 128), F32), [S, V], V,
        [pltpu.VMEM((most_h, 2, 128), F32), pltpu.VMEM((table_rows, 2, 128), F32)],
        first=0, count=most_h,
    )(wanted, grads_h)
    table_grad = call(
        scatter_last_kernel, "scatter_candidates", 18, shape((table_rows, col_width), F32), [S, V, V], V,
        [pltpu.VMEM((most_c, 2, 128), F32), pltpu.VMEM((128, 2, 128), F32)],
        first=most_h, count=most_c,
    )(wanted, grads_c, half)
    return (logits.reshape(1, cand), table_grad)


def solution(mesh):
    in_specs = (
        P("rows", None, None), P("rows", None), P("rows", None, None), P("rows", None), P("rows"),
        P("rows", "cols"), P(), P(), P(), P(("rows", "cols"), None),
    )
    out_specs = (P(("rows", "cols"), None), P("rows", "cols"))
    return jax.shard_map(body, mesh=mesh, in_specs=in_specs, out_specs=out_specs, check_vma=False)
```

profile of v0, /device:TPU:1, one launch (start us, length us, event | category | flops | bytes accessed | tf_op | source)
XLA Modules:
  0.0 281.9 jit_solution(2072878732793613018)
XLA Ops:
  3.5 3.4 %requests.1 = (s32[32,4,128]{2,1,0:T(4,128)S(1)}, s32[1,1024]{1,0:T(1,128)S(1)}, s32[1,512]{1,0:T(1,128)S(1)}) custom-call(s32[1]{0:T(128)} %bitcast.me, s32[4,1024]{1,0:T(4,128)S(1)} %bitcast.25, s32[4,1024]{1,0:T(4,128)S(1)} %copy-done.17, s32[4,512]{1,0:T(4,128)S(1)} %bitcast.26, s32[4,512]{1,0:T(4,128)S(1)} %copy-done.18), custom_call_target="tpu_custom_call" | custom-call | tf_op jit(solution)/shard_map/requests/pallas_call | solution.py:300
  6.9 15.7 %all_to_all.25 = s32[32,4,128]{2,1,0:T(4,128)S(1)} all-to-all(s32[32,4,128]{2,1,0:T(4,128)S(1)} %get-tuple-element.13), channel_id=1, replica_groups=mesh['rows'=32,'cols'=4] {'rows'}, dimensions={0} | all-to-all | bytes 131072 | tf_op jit(solution)/shard_map/all_to_all | solution.py:305
  24.2 9.0 %gather_rows.3 = bf16[128,48,128]{2,1,0:T(8,128)(2,1)S(1)} custom-call(s32[128,128]{1,0:T(8,128)S(1)} %bitcast.21, bf16[4096,256]{1,0:T(8,128)(2,1)S(1)} %copy-done.4), custom_call_target="tpu_custom_call" | custom-call | tf_op jit(solution)/shard_map/gather_rows/pallas_call | solution.py:319
  34.4 7.0 %all-to-all-start.2 = ((bf16[128,48,128]{2,1,0:T(8,128)(2,1)}), bf16[128,48,128]{2,1,0:T(8,128)(2,1)}, u32[]{:S(2)}, u32[]{:S(2)}) async-start(bf16[128,48,128]{2,1,0:T(8,128)(2,1)} %copy-done.6), calls=%async_computation.2 | async-start | bytes 3145728 | tf_op jit(solution)/shard_map/fetch_c/all_to_all | solution.py:317
  41.4 14.6 %gather_rows.2 = bf16[128,96,128]{2,1,0:T(8,128)(2,1)} custom-call(s32[128,128]{1,0:T(8,128)S(1)} %bitcast.22, bf16[4096,256]{1,0:T(8,128)(2,1)S(1)} %copy-done.5), custom_call_target="tpu_custom_call" | custom-call | tf_op jit(solution)/shard_map/gather_rows/pallas_call | solution.py:321
  56.0 10.2 %all-to-all-done.2 = bf16[128,48,128]{2,1,0:T(8,128)(2,1)} async-done(((bf16[128,48,128]{2,1,0:T(8,128)(2,1)}), bf16[128,48,128]{2,1,0:T(8,128)(2,1)}, u32[]{:S(2)}, u32[]{:S(2)}) %all-to-all-start.2) | async-done | bytes 1572896 | tf_op jit(solution)/shard_map/fetch_c/all_to_all | solution.py:317
  66.2 4.9 %all-to-all-start.1 = ((bf16[128,96,128]{2,1,0:T(8,128)(2,1)}), bf16[128,96,128]{2,1,0:T(8,128)(2,1)}, u32[]{:S(2)}, u32[]{:S(2)}) async-start(bf16[128,96,128]{2,1,0:T(8,128)(2,1)} %gather_rows.2), calls=%async_computation.1 | async-start | bytes 6291456 | tf_op jit(solution)/shard_map/fetch_h/all_to_all | solution.py:317
  71.7 3.3 %fusion.u_row = f32[1,1024]{1,0:T(1,128)S(1)} fusion(f32[1024,1]{0,1:T(1,128)S(1)} %bitcast.27, bf16[2,1024,1024]{2,1,0:T(8,128)(2,1)} %wo_in.1), kind=kOutput, calls=%fused_computation | convolution fusion | flops 12582912 | bytes 2105344 | tf_op jit(solution)/shard_map/score_row/dot_general | solution.py:325
  75.0 2.2 copy-done
  77.2 5.4 %prepare.1 = (bf16[1536,1024]{1,0:T(8,128)(2,1)S(1)}, bf16[1536,1024]{1,0:T(8,128)(2,1)S(1)}, bf16[512,1024]{1,0:T(8,128)(2,1)S(1)}, bf16[512,1024]{1,0:T(8,128)(2,1)S(1)}) custom-call(bf16[32,4,48,128]{3,2,1,0:T(8,128)(2,1)} %bitcast.3.recv, s32[1,1024]{1,0:T(1,128)S(1)} %get-tuple-element.14.h_pos, s32[1,512]{1,0:T(1,128)S(1)} %get-tuple-element.15.c_pos, ...), custom_call_target="tpu_custom_call" | custom-call | tf_op jit(solution)/shard_map/prepare/pallas_call | solution.py:328
  82.7 1.7 copy-done.8
  84.4 1.6 copy-done.9
  88.0 24.9 %all-to-all-done.1 = bf16[128,96,128]{2,1,0:T(8,128)(2,1)} async-done(((bf16[128,96,128]{2,1,0:T(8,128)(2,1)}), bf16[128,96,128]{2,1,0:T(8,128)(2,1)}, u32[]{:S(2)}, u32[]{:S(2)}) %all-to-all-start.1) | async-done | bytes 3145760 | tf_op jit(solution)/shard_map/fetch_h/all_to_all | solution.py:317
  112.9 63.2 %user_pass.1 = (bf16[32,4,96,128]{3,2,1,0:T(8,128)(2,1)}, bf16[512,1024]{1,0:T(8,128)(2,1)S(1)}, f32[512,1024]{1,0:T(8,128)}, f32[512,1]{1,0:T(8,128)S(1)}) custom-call(s32[1]{0:T(128)} %dynamic_slice.3.length, bf16[32,4,96,128]{3,2,1,0:T(8,128)(2,1)} %bitcast.2.recv_in, bf16[1536,1024]{1,0:T(8,128)(2,1)} %copy-done.8, bf16[512,1024]{1,0:T(8,128)(2,1)} %copy-done.12, ...), custom_call_target="tpu_custom_call" | custom-call | tf_op jit(solution)/shard_map/user_pass/pallas_call | solution.py:334
  177.1 3.9 %all-to-all-start.4 = ((bf16[128,96,128]{2,1,0:T(8,128)(2,1)}), bf16[128,96,128]{2,1,0:T(8,128)(2,1)S(1)}, u32[]{:S(2)}, u32[]{:S(2)}) async-start(bf16[128,96,128]{2,1,0:T(8,128)(2,1)} %bitcast.29), calls=%async_computation.4 | async-start | bytes 6291456 | tf_op jit(solution)/shard_map/return_h/all_to_all | solution.py:317
  181.0 2.2 copy-done.1
  183.1 1.9 copy-done.10
  187.8 3.2 %finish.1 = bf16[32,4,48,128]{3,2,1,0:T(8,128)(2,1)S(1)} custom-call(bf16[512,1024]{1,0:T(8,128)(2,1)S(1)} %copy-done.15, f32[512,1024]{1,0:T(8,128)S(1)} %copy-done.11, bf16[1536,1024]{1,0:T(8,128)(2,1)S(1)} %copy-done.10, bf16[2,1024,1024]{2,1,0:T(8,128)(2,1)S(1)} %copy-done.1), custom_call_target="tpu_custom_call" | custom-call | tf_op jit(solution)/shard_map/finish/pallas_call | solution.py:364
  192.2 30.9 %all-to-all-done.4.grads = bf16[128,96,128]{2,1,0:T(8,128)(2,1)S(1)} async-done(((bf16[128,96,128]{2,1,0:T(8,128)(2,1)}), bf16[128,96,128]{2,1,0:T(8,128)(2,1)S(1)}, u32[]{:S(2)}, u32[]{:S(2)}) %all-to-all-start.4) | async-done | bytes 3145760 | tf_op jit(solution)/shard_map/return_h/all_to_all | solution.py:317
  223.0 4.8 %all-to-all-start.3 = ((bf16[128,48,128]{2,1,0:T(8,128)(2,1)}), bf16[128,48,128]{2,1,0:T(8,128)(2,1)}, u32[]{:S(2)}, u32[]{:S(2)}) async-start(bf16[128,48,128]{2,1,0:T(8,128)(2,1)} %bitcast.20), calls=%async_computation.3 | async-start | bytes 3145728 | tf_op jit(solution)/shard_map/return_c/all_to_all | solution.py:317
  228.6 27.9 %scatter_history.1.start = f32[4096,2,128]{2,1,0:T(2,128)S(1)} custom-call(s32[128,128]{1,0:T(8,128)S(1)} %bitcast.23, bf16[128,96,128]{2,1,0:T(8,128)(2,1)S(1)} %all-to-all-done.4.grads), custom_call_target="tpu_custom_call" | custom-call | tf_op jit(solution)/shard_map/scatter_history/pallas_call | solution.py:369
  256.5 2.0 copy-done.2
  258.5 2.2 copy-done.3
  260.7 21.2 %scatter_candidates.1 = f32[4096,256]{1,0:T(8,128)} custom-call(s32[128,128]{1,0:T(8,128)S(1)} %bitcast.24, bf16[128,48,128]{2,1,0:T(8,128)(2,1)} %all-to-all-done.3.grads, f32[4096,2,128]{2,1,0:T(2,128)S(1)} %copy-done.3), custom_call_target="tpu_custom_call" | custom-call | tf_op jit(solution)/shard_map/scatter_candidates/pallas_call | solution.py:374
  (40 shorter events, 13.8 us)
Async XLA Ops:
  2.1 0.7 copy-start.17
  22.6 1.6 copy-start.4
  24.2 17.2 %copy-start.5 = (bf16[4096,256]{1,0:T(8,128)(2,1)S(1)}, bf16[4096,256]{1,0:T(8,128)(2,1)}, u32[]{:S(2)}) copy-start(bf16[4096,256]{1,0:T(8,128)(2,1)} %table.3) | copy-start | bytes 6291460
  33.2 1.1 copy-start.6
  34.4 31.9 %all-to-all-start.2 = ((bf16[128,48,128]{2,1,0:T(8,128)(2,1)}), bf16[128,48,128]{2,1,0:T(8,128)(2,1)}, u32[]{:S(2)}, u32[]{:S(2)}) async-start(bf16[128,48,128]{2,1,0:T(8,128)(2,1)} %copy-done.6), calls=%async_computation.2 | async-start | bytes 3145728 | tf_op jit(solution)/shard_map/fetch_c/all_to_all | solution.py:317
  56.0 15.1 %copy-start.20 = (s32[4]{0:T(128)S(1)}, s32[4]{0:T(128)}, u32[]{:S(2)}) copy-start(s32[4]{0:T(128)} %param.14) | copy-start | bytes 52
  56.0 15.7 %copy-start.16 = (f32[1024]{0:T(1024)S(1)}, f32[1024]{0:T(1024)}, u32[]{:S(2)}) copy-start(f32[1024]{0:T(1024)} %param.18) | copy-start | bytes 12292
  66.2 46.7 %all-to-all-start.1 = ((bf16[128,96,128]{2,1,0:T(8,128)(2,1)}), bf16[128,96,128]{2,1,0:T(8,128)(2,1)}, u32[]{:S(2)}, u32[]{:S(2)}) async-start(bf16[128,96,128]{2,1,0:T(8,128)(2,1)} %gather_rows.2), calls=%async_computation.1 | async-start | bytes 6291456 | tf_op jit(solution)/shard_map/fetch_h/all_to_all | solution.py:317
  75.0 37.9 %copy-start.19 = (f32[1,512]{1,0:T(1,128)S(1)}, f32[1,512]{1,0:T(1,128)}, u32[]{:S(2)}) copy-start(f32[1,512]{1,0:T(1,128)} %lg_row.1) | copy-start | bytes 6148
  75.0 2.2 copy-start
  82.7 1.7 copy-start.8
  84.4 1.6 copy-start.9
  86.0 1.0 copy-start.12
  87.0 1.0 copy-start.13
  176.1 1.0 copy-start.14
  177.1 46.0 %all-to-all-start.4 = ((bf16[128,96,128]{2,1,0:T(8,128)(2,1)}), bf16[128,96,128]{2,1,0:T(8,128)(2,1)S(1)}, u32[]{:S(2)}, u32[]{:S(2)}) async-start(bf16[128,96,128]{2,1,0:T(8,128)(2,1)} %bitcast.29), calls=%async_computation.4 | async-start | bytes 6291456 | tf_op jit(solution)/shard_map/return_h/all_to_all | solution.py:317
  180.9 2.2 copy-start.1
  183.1 1.9 copy-start.10
  185.0 1.6 copy-start.11
  186.6 1.2 copy-start.15
  191.0 1.1 copy-start.7
  223.0 35.5 %all-to-all-start.3 = ((bf16[128,48,128]{2,1,0:T(8,128)(2,1)}), bf16[128,48,128]{2,1,0:T(8,128)(2,1)}, u32[]{:S(2)}, u32[]{:S(2)}) async-start(bf16[128,48,128]{2,1,0:T(8,128)(2,1)} %bitcast.20), calls=%async_computation.3 | async-start | bytes 3145728 | tf_op jit(solution)/shard_map/return_c/all_to_all | solution.py:317
  256.5 2.0 copy-start.2
  258.5 2.2 copy-start.3
  (1 other events, 0.7 us)
where the time goes:
time: 287 us; the launch traced here: 282 us
  Pallas kernels  148 us (52%)
  waiting for transfers between devices  66 us (23%)
  local copies, waits for them, and re-layouts  26.9 us (9%)
  starting transfers between devices  20.5 us (7%)
  blocking collectives  15.7 us (5%)
  matrix products  3.31 us (1%)
    all_to_all x4, waiting for transfers between devices, exchange(): lax.all_to_all(x, ('rows', 'cols'), split_axis=0, concat_axis=0, tiled=True)  66 us
    pallas_call x1, Pallas kernels, body(): call(user_kernel, 'user_pass', 52, (shape((n_rows, n_cols, 2 * most_h, 12...  63.2 us
    pallas_call x1, Pallas kernels, body(): call(scatter_first_kernel, 'scatter_history', 18, shape((table_rows, 2, 1...  27.9 us
    unnamed x44, local copies, waits for them, and re-layouts  26.3 us
    pallas_call x1, Pallas kernels, body(): call(scatter_last_kernel, 'scatter_candidates', 18, shape((table_rows, co...  21.2 us
    all_to_all x4, starting transfers between devices, exchange(): lax.all_to_all(x, ('rows', 'cols'), split_axis=0, concat_axis=0, tiled=True)  20.5 us
    all_to_all x1, blocking collectives, body(): lax.all_to_all(req, 'rows', split_axis=0, concat_axis=0, tiled=True)  15.7 us
    pallas_call x1, Pallas kernels, body(): found_h = gather(0, most_h)(wanted, embed_table)  14.6 us
  transfers between devices with their start and end apart: 4, of which 3 were waited for; matrix products, arithmetic and copies ran while one was open for 2% of the time, Pallas kernels for 18%

commit v1 on v0

v1 whole, which is shorter than its diff:
```python
import functools
import math

import jax
import jax.numpy as jnp
from jax import lax
from jax.experimental import pallas as pl
from jax.experimental.pallas import tpu as pltpu
from jax.sharding import PartitionSpec as P

HEADS = 8
BF = jnp.bfloat16
F32 = jnp.float32
NN = (((1,), (0,)), ((), ()))
NT = (((1,), (1,)), ((), ()))
TN = (((0,), (0,)), ((), ()))
VMEM_SPEC = pl.BlockSpec(memory_space=pltpu.VMEM)
SMEM_SPEC = pl.BlockSpec(memory_space=pltpu.SMEM)
MIB = 1024 * 1024


def dot(a, b, dims):
    return lax.dot_general(a, b, dims, preferred_element_type=F32)


def iota(shape, axis):
    return lax.broadcasted_iota(jnp.int32, shape, axis)


def request_kernel(me, h_own, h_row, c_own, c_row, req, h_pos, c_pos, *, rows, most_h, most_c):
    users, hist = h_own.shape
    cand = c_own.shape[1]
    before = (iota((hist, hist), 0) < iota((hist, hist), 1)).astype(BF)
    for u in range(users):
        parts = []
        for own, row, base, most, pos in (
            (h_own, h_row, 0, most_h, h_pos),
            (c_own, c_row, most_h, most_c, c_pos),
        ):
            n = own.shape[1]
            owner = own[u : u + 1, :]
            match = (iota((rows, n), 0) == owner).astype(F32)
            earlier = dot(match.astype(BF), before[:n, :n], NN)
            rank = jnp.sum(match * earlier, axis=0, keepdims=True).astype(jnp.int32)

            @pl.when(me[0] == u)
            def _():
                pos[...] = owner * 48 + rank

            ids = row[u : u + 1, :]
            high = (match * (ids >> 6).astype(F32)).astype(BF)
            low = (match * (ids & 63).astype(F32)).astype(BF)
            hit = (iota((128, n), 0) == rank + base).astype(BF)
            parts.append(dot(jnp.concatenate([high, low], axis=0), hit, NT))
        both = parts[0] + parts[1]
        req[:, u, :] = (both[:rows] * 64.0 + both[rows:]).astype(jnp.int32)


def gather_kernel(idx, table, out, wide, stage, *, most_h):
    n_rows = table.shape[0]
    count = stage.shape[0]
    chunk = 256
    flat = wide.reshape(2 * n_rows, 128)
    lines = stage.reshape(2 * count, 128)

    def widen(i, carry):
        at = pl.multiple_of(i * chunk, chunk)
        block = table[pl.ds(at, chunk), :].astype(F32)
        flat[pl.ds(2 * at, chunk, stride=2), :] = block[:, :128]
        flat[pl.ds(2 * at + 1, chunk, stride=2), :] = block[:, 128:]
        return carry

    lax.fori_loop(0, n_rows // chunk, widen, 0)

    def fetch(u, carry):
        for s in range(count):
            stage[s] = wide[idx[u, s]]
        out[u, 0:most_h, :] = lines[pl.ds(0, most_h, stride=2), :].astype(BF)
        out[u, most_h : 2 * most_h, :] = lines[pl.ds(1, most_h, stride=2), :].astype(BF)
        tail = [lines[pl.ds(2 * most_h + half, count - most_h, stride=2), :] for half in range(2)]
        out[u, 2 * most_h :, :] = jnp.concatenate(tail, axis=0).astype(BF)
        return carry

    lax.fori_loop(0, out.shape[0], fetch, 0)


def scatter_kernel(idx, grads, out, stage, *sums, most_h):
    count = stage.shape[0]
    lines = stage.reshape(2 * count, 128)
    for total in sums:
        total[...] = jnp.zeros_like(total)

    def add(u, carry):
        block = grads[u].astype(F32)
        lines[pl.ds(0, most_h, stride=2), :] = block[:most_h]
        lines[pl.ds(1, most_h, stride=2), :] = block[most_h : 2 * most_h]
        lines[pl.ds(2 * most_h, count - most_h, stride=2), :] = block[2 * most_h : most_h + count]
        lines[pl.ds(2 * most_h + 1, count - most_h, stride=2), :] = block[most_h + count :]
        for s in range(count):
            total = sums[s % len(sums)]
            at = idx[u, s]
            total[at] = total[at] + stage[s]
        return carry

    lax.fori_loop(0, grads.shape[0], add, 0)
    chunk = 128
    flats = [total.reshape(2 * out.shape[0], 128) for total in sums]

    def finish(i, carry):
        at = pl.multiple_of(i * chunk, chunk)
        for half in range(2):
            from_rows = pl.ds(2 * at + half, chunk, stride=2)
            total = flats[0][from_rows, :]
            for flat in flats[1:]:
                total = total + flat[from_rows, :]
            out[pl.ds(at, chunk), half * 128 : half * 128 + 128] = total
        return carry

    lax.fori_loop(0, out.shape[0] // chunk, finish, 0)


def user_kernel(
    length, recv_in, wq_in, wo_in, h_pos, c_pos, lg_row, sw, u_row,
    send_out, logits,
    recv, pt_h, pt_c, cand, q1, wq, wo0, keys, q2, att1, soft, d_keys, d_q, d_att, d_stream, in_sems, out_sems,
):
    hist = keys.shape[0]
    n_cand = cand.shape[0]
    rows, cols = recv_in.shape[0], recv_in.shape[1]
    slots = pt_h.shape[0]
    inv_root = 1.0 / math.sqrt(128)
    blocks = [slice(at, at + 256) for at in range(0, n_cand, 256)]
    whole = [slice(0, n_cand)]
    pairs = [(recv_in.at[:, c], recv.at[c]) for c in range(cols)]
    pairs += [(wq_in, wq), (wo_in.at[0], wo0)]
    loads = [pltpu.make_async_copy(src, dst, in_sems.at[i]) for i, (src, dst) in enumerate(pairs)]
    for load in loads:
        load.start()
    for at in range(0, slots, 256):
        place = iota((256, hist), 0) + at
        pt_h[at : at + 256, :] = jnp.where(place == h_pos[...], 1.0, 0.0).astype(BF)
        place = iota((256, n_cand), 0) + at
        pt_c[at : at + 256, 0:n_cand] = jnp.where(place == c_pos[...], 1.0, 0.0).astype(BF)
        pt_c[at : at + 256, n_cand:] = jnp.where(place == c_pos[...] + 24, 1.0, 0.0).astype(BF)

    def slab(c, part):
        return recv[c, :, part[0] : part[1], :].reshape(slots, 128)

    hist_even, hist_odd, cands = (0, 48), (48, 96), (96, 144)
    for c in range(cols):
        loads[c].wait()
        both = jnp.concatenate([slab(c, hist_even), slab(c, hist_odd)], axis=1)
        keys[:, c * 256 : c * 256 + 256] = dot(pt_h[...], both, TN).astype(BF)
        if c % 2:
            got = dot(pt_c[...], jnp.concatenate([slab(c - 1, cands), slab(c, cands)], axis=1), TN).astype(BF)
            for k in range(2):
                at = (c - 1 + k) * 256
                cand[:, at : at + 128] = got[:n_cand, k * 128 : k * 128 + 128]
                cand[:, at + 128 : at + 256] = got[n_cand:, k * 128 : k * 128 + 128]
    for load in loads[cols:]:
        load.wait()
    q1[...] = dot(cand[...], wq[0], NN).astype(BF)

    lg = jnp.transpose(jnp.broadcast_to(lg_row[...], (8, n_cand)))[:, 0:1]
    bias = jnp.where(iota((1, hist), 1) < length[0], 0.0, -1e30)
    scale = inv_root * math.log2(math.e)

    def softmax(scores):
        scores = scores + bias
        top = jnp.max(scores, axis=1, keepdims=True)
        e = jnp.exp2((scores - top) * scale)
        return e * (1.0 / jnp.sum(e, axis=1, keepdims=True))

    def first_layer(h, carry):
        hs = pl.ds(pl.multiple_of(h * 128, 128), 128)
        k = keys[:, hs]
        scores = [dot(q1[b, hs], k, NT) for b in blocks]
        for b, s in zip(blocks, scores):
            y = softmax(s)
            soft[h, b, :] = y
            att1[b, hs] = dot(y.astype(BF), k, NN).astype(BF)
        return carry

    lax.fori_loop(0, HEADS, first_layer, 0)
    stream = cand[...].astype(F32) + dot(att1[...], wo0[...], NN)
    q2[...] = dot(stream.astype(BF), wq[1], NN).astype(BF)
    score = jnp.sum(stream * sw[...], axis=1, keepdims=True)
    lgs = lg * inv_root

    def second_layer(h, score):
        hs = pl.ds(pl.multiple_of(h * 128, 128), 128)
        k = keys[:, hs]
        u = u_row[:, hs]
        u_hi = u.astype(BF).astype(F32)
        u_mid = (u - u_hi).astype(BF).astype(F32)
        u_low = u - u_hi - u_mid
        line = iota((16, 128), 0)
        pieces = jnp.where(line == 0, u_hi, jnp.where(line == 1, u_mid, jnp.where(line == 2, u_low, 0.0)))
        g = jnp.sum(dot(pieces.astype(BF), k, NT), axis=0, keepdims=True)
        scores = [dot(q2[b, hs], k, NT) for b in whole]
        ws, dss = [], []
        for b, s in zip(whole, scores):
            y = softmax(s)
            w = y.astype(BF)
            mean = jnp.sum(y * g, axis=1, keepdims=True)
            ds = (y * lgs[b] * (g - mean)).astype(BF)
            ws.append(w)
            dss.append(ds)
            d_stream[b, hs] = dot(w, k, NN).astype(BF).astype(F32) * u
            d_q[b, hs] = dot(ds, k, NN).astype(BF)
        ds = jnp.concatenate(dss, axis=0)
        w = jnp.concatenate(ws, axis=0)
        d_keys[:, hs] = dot(ds, q2[:, hs], TN) + dot(w, (lg * u).astype(BF), TN)
        return score

    lax.fori_loop(0, HEADS, second_layer, 0)
    score = score + jnp.sum(d_stream[...], axis=1, keepdims=True)
    logits[...] = jnp.transpose(jnp.broadcast_to(score, (n_cand, 128)))[0:1, :]
    d_after = lg * sw[...] + dot(d_q[...], wq[1], NT).astype(BF).astype(F32)
    d_stream[...] = d_after
    d_att[...] = dot(d_after.astype(BF), wo0[...], NT).astype(BF)

    def first_back(h, carry):
        hs = pl.ds(pl.multiple_of(h * 128, 128), 128)
        k = keys[:, hs]
        slopes = [dot(d_att[b, hs], k, NT) for b in blocks]
        total = d_keys[:, hs]
        for b, dw in zip(blocks, slopes):
            y = soft[h, b, :]
            mean = jnp.sum(y * dw, axis=1, keepdims=True)
            ds = (y * (dw - mean)).astype(BF)
            d_q[b, hs] = (dot(ds, k, NN) * inv_root).astype(BF)
            total = total + dot(ds, q1[b, hs], TN) * inv_root + dot(y.astype(BF), d_att[b, hs], TN)
        keys[:, hs] = total.astype(BF)
        return carry

    lax.fori_loop(0, HEADS, first_back, 0)
    att1[...] = (d_stream[...] + dot(d_q[...], wq[0], NT).astype(BF).astype(F32)).astype(BF)
    puts = []
    for c in range(cols):
        if c % 2 == 0:
            at = c * 256
            even = jnp.concatenate([att1[:, at : at + 128], att1[:, at + 256 : at + 384]], axis=1)
            odd = jnp.concatenate([att1[:, at + 128 : at + 256], att1[:, at + 384 : at + 512]], axis=1)
            got = dot(pt_c[...], jnp.concatenate([even, odd], axis=0), NN).astype(BF)
            recv[c, :, cands[0] : cands[1], :] = got[:, :128].reshape(rows, 48, 128)
            recv[c + 1, :, cands[0] : cands[1], :] = got[:, 128:].reshape(rows, 48, 128)
        got = dot(pt_h[...], keys[:, c * 256 : c * 256 + 256], NN).astype(BF)
        recv[c, :, hist_even[0] : hist_even[1], :] = got[:, :128].reshape(rows, 48, 128)
        recv[c, :, hist_odd[0] : hist_odd[1], :] = got[:, 128:].reshape(rows, 48, 128)
        put = pltpu.make_async_copy(recv.at[c], send_out.at[:, c], out_sems.at[c])
        put.start()
        puts.append(put)
    for put in puts:
        put.wait()


def call(kernel, name, mib, out_shape, in_specs, out_specs, scratch=(), **static):
    return pl.pallas_call(
        functools.partial(kernel, **static),
        out_shape=out_shape,
        in_specs=in_specs,
        out_specs=out_specs,
        scratch_shapes=list(scratch),
        compiler_params=pltpu.CompilerParams(vmem_limit_bytes=mib * MIB),
        name=name,
    )


def shape(dims, kind):
    return jax.ShapeDtypeStruct(dims, kind)


def body(
    history_owner, history_row, candidate_owner, candidate_row, history_length,
    embed_table, query_weight, output_weight, score_weight, logit_grad,
):
    n_rows = lax.axis_size("rows")
    n_cols = lax.axis_size("cols")
    users, hist = history_row.shape
    cand = candidate_row.shape[1]
    most_h = 3 * hist // (2 * n_rows)
    most_c = 3 * cand // (2 * n_rows)
    table_rows, col_width = embed_table.shape
    width = n_cols * col_width
    peers = n_rows * n_cols
    slots = n_rows * most_h
    me = lax.axis_index("cols").astype(jnp.int32)
    V, S, A = VMEM_SPEC, SMEM_SPEC, pl.BlockSpec(memory_space=pl.ANY)
    req, h_pos, c_pos = call(
        request_kernel, "requests", 16,
        (shape((n_rows, users, 128), jnp.int32), shape((1, hist), jnp.int32), shape((1, cand), jnp.int32)),
        [S, V, V, V, V], (V, V, V), rows=n_rows, most_h=most_h, most_c=most_c,
    )(me.reshape(1), history_owner[:, :, 0], history_row, candidate_owner[:, :, 0], candidate_row)
    wanted = lax.all_to_all(req, "rows", split_axis=0, concat_axis=0, tiled=True)
    wanted = wanted.reshape(peers, 128)

    def exchange(x):
        return lax.all_to_all(x, ("rows", "cols"), split_axis=0, concat_axis=0, tiled=True)

    count = most_h + most_c
    found = call(
        gather_kernel, "gather_rows", 24, shape((peers, 2 * count, 128), BF), [S, V], V,
        [pltpu.VMEM((table_rows, 2, 128), F32), pltpu.VMEM((count, 2, 128), F32)], most_h=most_h,
    )(wanted, embed_table)
    back = exchange(found)
    length = lax.dynamic_slice_in_dim(history_length, me, 1)
    u_row = jnp.dot(
        output_weight[1].astype(F32), score_weight, precision=lax.Precision.HIGHEST
    ).reshape(1, -1)
    send, logits = call(
        user_kernel, "user_pass", 60,
        (shape((n_rows, n_cols, 2 * count, 128), BF), shape((1, cand), F32)),
        [S, A, A, A, V, V, V, V, V], (A, V),
        [
            pltpu.VMEM((n_cols, n_rows, 2 * count, 128), BF),
            pltpu.VMEM((slots, hist), BF),
            pltpu.VMEM((slots, 2 * cand), BF),
            pltpu.VMEM((cand, width), BF),
            pltpu.VMEM((cand, width), BF),
            pltpu.VMEM(query_weight.shape, BF),
            pltpu.VMEM((width, width), BF),
            pltpu.VMEM((hist, width), BF),
            pltpu.VMEM((cand, width), BF),
            pltpu.VMEM((cand, width), BF),
            pltpu.VMEM((HEADS, cand, hist), F32),
            pltpu.VMEM((hist, width), F32),
            pltpu.VMEM((cand, width), BF),
            pltpu.VMEM((cand, width), BF),
            pltpu.VMEM((cand, width), F32),
            pltpu.SemaphoreType.DMA((2 + n_cols,)),
            pltpu.SemaphoreType.DMA((n_cols,)),
        ],
    )(
        length, back.reshape(n_rows, n_cols, 2 * count, 128), query_weight, output_weight,
        h_pos, c_pos, logit_grad, score_weight.reshape(1, -1), u_row,
    )
    grads = exchange(send.reshape(peers, 2 * count, 128))
    table_grad = call(
        scatter_kernel, "scatter_rows", 32, shape((table_rows, col_width), F32), [S, V], V,
        [pltpu.VMEM((count, 2, 128), F32)] + [pltpu.VMEM((table_rows, 2, 128), F32)] * 2, most_h=most_h,
    )(wanted, grads)
    return (logits, table_grad)


def solution(mesh):
    in_specs = (
        P("rows", None, None), P("rows", None), P("rows", None, None), P("rows", None), P("rows"),
        P("rows", "cols"), P(), P(), P(), P(("rows", "cols"), None),
    )
    out_specs = (P(("rows", "cols"), None), P("rows", "cols"))
    return jax.shard_map(body, mesh=mesh, in_specs=in_specs, out_specs=out_specs, check_vma=False)
```

time: 287 us -> 267 us (0.930); the launches traced: 282 us -> 266 us
  blocking collectives: 15.7 us -> 78.8 us
  Pallas kernels: 148 us -> 115 us
  local copies, waits for them, and re-layouts: 26.9 us -> 7.26 us
  starting transfers between devices: 20.5 us -> 7.04 us
  waiting for transfers between devices: 66 us -> 54 us
    all_to_all x0 -> x1, blocking collectives: none -> 63.1 us  [exchange(): lax.all_to_all(x, ('rows', 'cols'), split_axis=0, concat_axis=0, tiled=True)]
    pallas_call x7 -> x3, Pallas kernels: 145 us -> 111 us  [the longest x1 66.3 us: body(): call(user_kernel, 'user_pass', 60, (shape((n_rows, n_cols, 2 * count, 128...]
    unnamed x44 -> x18, local copies, waits for them, and re-layouts: 26.3 us -> 6.62 us
    all_to_all x4 -> x1, starting transfers between devices: 20.5 us -> 7.04 us  [exchange(): lax.all_to_all(x, ('rows', 'cols'), split_axis=0, concat_axis=0, tiled=True)]
    all_to_all x4 -> x1, waiting for transfers between devices: 66 us -> 54 us  [exchange(): lax.all_to_all(x, ('rows', 'cols'), split_axis=0, concat_axis=0, tiled=True)]
  transfers between devices with their start and end apart: 4 -> 1, of which waited for: 3 -> 1; matrix products, arithmetic and copies ran while one was open for 2% -> 2% of each run, Pallas kernels for 18% -> 0%
where the time goes in v1:
time: 267 us; the launch traced here: 266 us
  Pallas kernels  115 us (43%)
  blocking collectives  78.8 us (30%)
  waiting for transfers between devices  54 us (20%)
  local copies, waits for them, and re-layouts  7.26 us (3%)
  starting transfers between devices  7.04 us (3%)
  matrix products  3.92 us (1%)
    pallas_call x1, Pallas kernels, body(): call(user_kernel, 'user_pass', 60, (shape((n_rows, n_cols, 2 * count, 128...  66.3 us
    all_to_all x1, blocking collectives, exchange(): lax.all_to_all(x, ('rows', 'cols'), split_axis=0, concat_axis=0, tiled=True)  63.1 us
    all_to_all x1, waiting for transfers between devices, exchange(): lax.all_to_all(x, ('rows', 'cols'), split_axis=0, concat_axis=0, tiled=True)  54 us
    pallas_call x1, Pallas kernels, body(): call(scatter_kernel, 'scatter_rows', 32, shape((table_rows, col_width), F...  32.4 us
    all_to_all x1, blocking collectives, body(): lax.all_to_all(req, 'rows', split_axis=0, concat_axis=0, tiled=True)  15.7 us
    pallas_call x1, Pallas kernels, body(): call(gather_kernel, 'gather_rows', 24, shape((peers, 2 * count, 128), BF)...  12.6 us
    all_to_all x1, starting transfers between devices, exchange(): lax.all_to_all(x, ('rows', 'cols'), split_axis=0, concat_axis=0, tiled=True)  7.04 us
    unnamed x18, local copies, waits for them, and re-layouts  6.62 us
  transfers between devices with their start and end apart: 1, of which 1 were waited for; matrix products, arithmetic and copies ran while one was open for 2% of the time, Pallas kernels for 0%

profile of v1, /device:TPU:1, one launch (start us, length us, event | category | flops | bytes accessed | tf_op | source)
XLA Modules:
  0.0 266.4 jit_solution(10725413912297308094)
XLA Ops:
  0.6 0.7 copy.16
  1.4 0.7 copy.17
  2.1 0.0 copy-start.2
  2.1 0.7 copy-done.2
  2.8 0.7 copy-done.3
  3.5 3.4 %requests.1 = (s32[32,4,128]{2,1,0:T(4,128)S(1)}, s32[1,1024]{1,0:T(1,128)S(1)}, s32[1,512]{1,0:T(1,128)S(1)}) custom-call(s32[1]{0:T(128)} %bitcast.me, s32[4,1024]{1,0:T(4,128)S(1)} %bitcast.19, s32[4,1024]{1,0:T(4,128)S(1)} %copy-done.2, s32[4,512]{1,0:T(4,128)S(1)} %bitcast.20, s32[4,512]{1,0:T(4,128)S(1)} %copy-done.3), custom_call_target="tpu_custom_call" | custom-call | tf_op jit(solution)/shard_map/requests/pallas_call | solution.py:290
  6.9 0.0 copy-start.4
  6.9 0.0 copy-start.5
  6.9 15.7 %all_to_all.15 = s32[32,4,128]{2,1,0:T(4,128)S(1)} all-to-all(s32[32,4,128]{2,1,0:T(4,128)S(1)} %get-tuple-element.7), channel_id=1, replica_groups=mesh['rows'=32,'cols'=4] {'rows'}, dimensions={0} | all-to-all | bytes 131072 | tf_op jit(solution)/shard_map/all_to_all | solution.py:295
  22.6 0.0 copy-done.4
  22.6 0.0 copy-done.5
  22.6 1.6 copy-done.1
  24.2 12.6 %gather_rows.1 = bf16[128,144,128]{2,1,0:T(8,128)(2,1)S(1)} custom-call(s32[128,128]{1,0:T(8,128)S(1)} %bitcast.17, bf16[4096,256]{1,0:T(8,128)(2,1)S(1)} %copy-done.1), custom_call_target="tpu_custom_call" | custom-call | tf_op jit(solution)/shard_map/gather_rows/pallas_call | solution.py:302
  36.9 0.0 copy-start
  36.9 2.2 copy-done
  39.1 7.0 %all-to-all-start.1 = ((bf16[128,144,128]{2,1,0:T(8,128)(2,1)}), bf16[128,144,128]{2,1,0:T(8,128)(2,1)}, u32[]{:S(2)}, u32[]{:S(2)}) async-start(bf16[128,144,128]{2,1,0:T(8,128)(2,1)} %copy-done), calls=%async_computation.1 | async-start | bytes 9437184 | tf_op jit(solution)/shard_map/all_to_all | solution.py:299
  46.1 0.0 copy-done.7
  46.1 0.6 dynamic_slice.3.length
  46.8 0.0 copy-done.6
  46.8 3.9 %fusion.u_row = f32[1,1024]{1,0:T(1,128)} fusion(f32[1024,1]{0,1:T(1,128)S(1)} %bitcast.23, bf16[2,1024,1024]{2,1,0:T(8,128)(2,1)} %wo_in.1), kind=kOutput, calls=%fused_computation | convolution fusion | flops 12582912 | bytes 2105344 | tf_op jit(solution)/shard_map/dot_general | solution.py:308
  50.7 54.0 %all-to-all-done.1 = bf16[128,144,128]{2,1,0:T(8,128)(2,1)} async-done(((bf16[128,144,128]{2,1,0:T(8,128)(2,1)}), bf16[128,144,128]{2,1,0:T(8,128)(2,1)}, u32[]{:S(2)}, u32[]{:S(2)}) %all-to-all-start.1) | async-done | bytes 4718624 | tf_op jit(solution)/shard_map/all_to_all | solution.py:299
  104.7 66.3 %user_pass.1 = (bf16[32,4,144,128]{3,2,1,0:T(8,128)(2,1)}, f32[1,512]{1,0:T(1,128)}) custom-call(s32[1]{0:T(128)} %dynamic_slice.3.length, bf16[32,4,144,128]{3,2,1,0:T(8,128)(2,1)} %bitcast.2.recv_in, bf16[2,1024,1024]{2,1,0:T(8,128)(2,1)} %wq_in.1, bf16[2,1024,1024]{2,1,0:T(8,128)(2,1)} %wo_in.1, s32[1,1024]{1,0:T(1,128)} %copy-done.4, ...), custom_call_target="tpu_custom_call" | custom-call | tf_op jit(solution)/shard_map/user_pass/pallas_call | solution.py:311
  171.0 63.1 %all_to_all.16.grads = bf16[128,144,128]{2,1,0:T(8,128)(2,1)S(1)} all-to-all(bf16[128,144,128]{2,1,0:T(8,128)(2,1)} %bitcast.21), channel_id=1, replica_groups=mesh['rows'=32,'cols'=4] {'rows','cols'}, dimensions={0} | all-to-all | bytes 9437184 | tf_op jit(solution)/shard_map/all_to_all | solution.py:299
  234.0 32.4 %scatter_rows.1 = f32[4096,256]{1,0:T(8,128)} custom-call(s32[128,128]{1,0:T(8,128)S(1)} %bitcast.18, bf16[128,144,128]{2,1,0:T(8,128)(2,1)S(1)} %all_to_all.16.grads), custom_call_target="tpu_custom_call" | custom-call | tf_op jit(solution)/shard_map/scatter_rows/pallas_call | solution.py:339
  (4 shorter events, 0.0 us)
Async XLA Ops:
  2.1 0.7 copy-start.2
  2.8 0.7 copy-start.3
  6.9 15.8 %copy-start.4 = (s32[1,1024]{1,0:T(1,128)}, s32[1,1024]{1,0:T(1,128)S(1)}, u32[]{:S(2)}) copy-start(s32[1,1024]{1,0:T(1,128)S(1)} %get-tuple-element.8.h_pos) | copy-start | bytes 12292
  6.9 15.8 %copy-start.5 = (s32[1,512]{1,0:T(1,128)}, s32[1,512]{1,0:T(1,128)S(1)}, u32[]{:S(2)}) copy-start(s32[1,512]{1,0:T(1,128)S(1)} %get-tuple-element.9.c_pos) | copy-start | bytes 6148
  22.6 1.6 copy-start.1
  36.9 2.2 copy-start
  39.1 7.1 %copy-start.7 = (s32[4]{0:T(128)S(1)}, s32[4]{0:T(128)}, u32[]{:S(2)}) copy-start(s32[4]{0:T(128)} %param.14) | copy-start | bytes 52
  39.1 7.7 %copy-start.6 = (f32[1024]{0:T(1024)S(1)}, f32[1024]{0:T(1024)}, u32[]{:S(2)}) copy-start(f32[1024]{0:T(1024)} %param.18) | copy-start | bytes 12292
  39.1 65.6 %all-to-all-start.1 = ((bf16[128,144,128]{2,1,0:T(8,128)(2,1)}), bf16[128,144,128]{2,1,0:T(8,128)(2,1)}, u32[]{:S(2)}, u32[]{:S(2)}) async-start(bf16[128,144,128]{2,1,0:T(8,128)(2,1)} %copy-done), calls=%async_computation.1 | async-start | bytes 9437184 | tf_op jit(solution)/shard_map/all_to_all | solution.py:299

commit v2 on v1

--- a/solution.py
+++ b/solution.py
@@ -27,18 +27,23 @@
     return lax.broadcasted_iota(jnp.int32, shape, axis)
 
 
-def request_kernel(me, h_own, h_row, c_own, c_row, req, h_pos, c_pos, *, rows, most_h, most_c):
-    users, hist = h_own.shape
-    cand = c_own.shape[1]
+def request_kernel(me, h_own_in, h_row_in, c_own_in, c_row_in, req, h_pos, c_pos, h_own, h_row, c_own, c_row, sems, *, rows, most_h, most_c):
+    pairs = ((h_own_in, h_own), (c_own_in, c_own), (h_row_in, h_row), (c_row_in, c_row))
+    loads = [pltpu.make_async_copy(src, dst, sems.at[i]) for i, (src, dst) in enumerate(pairs)]
+    for load in loads:
+        load.start()
+    users, hist = h_row.shape
     before = (iota((hist, hist), 0) < iota((hist, hist), 1)).astype(BF)
+    for load in loads:
+        load.wait()
     for u in range(users):
         parts = []
         for own, row, base, most, pos in (
             (h_own, h_row, 0, most_h, h_pos),
             (c_own, c_row, most_h, most_c, c_pos),
         ):
-            n = own.shape[1]
-            owner = own[u : u + 1, :]
+            n = row.shape[1]
+            owner = own[u]
             match = (iota((rows, n), 0) == owner).astype(F32)
             earlier = dot(match.astype(BF), before[:n, :n], NN)
             rank = jnp.sum(match * earlier, axis=0, keepdims=True).astype(jnp.int32)
@@ -56,12 +61,19 @@
         req[:, u, :] = (both[:rows] * 64.0 + both[rows:]).astype(jnp.int32)
 
 
-def gather_kernel(idx, table, out, wide, stage, *, most_h):
+def gather_kernel(idx, table_in, out, table, wide, stage, send, in_sems, out_sems, *, most_h):
     n_rows = table.shape[0]
     count = stage.shape[0]
+    pieces = 4
     chunk = 256
     flat = wide.reshape(2 * n_rows, 128)
     lines = stage.reshape(2 * count, 128)
+    part = n_rows // pieces
+    loads = []
+    for i in range(pieces):
+        at = pl.ds(i * part, part)
+        loads.append(pltpu.make_async_copy(table_in.at[at], table.at[at], in_sems.at[i]))
+        loads[i].start()
 
     def widen(i, carry):
         at = pl.multiple_of(i * chunk, chunk)
@@ -70,23 +82,41 @@
         flat[pl.ds(2 * at + 1, chunk, stride=2), :] = block[:, 128:]
         return carry
 
-    lax.fori_loop(0, n_rows // chunk, widen, 0)
+    for i in range(pieces):
+        loads[i].wait()
+        lax.fori_loop(i * part // chunk, (i + 1) * part // chunk, widen, 0)
 
     def fetch(u, carry):
         for s in range(count):
             stage[s] = wide[idx[u, s]]
-        out[u, 0:most_h, :] = lines[pl.ds(0, most_h, stride=2), :].astype(BF)
-        out[u, most_h : 2 * most_h, :] = lines[pl.ds(1, most_h, stride=2), :].astype(BF)
+        send[u, 0:most_h, :] = lines[pl.ds(0, most_h, stride=2), :].astype(BF)
+        send[u, most_h : 2 * most_h, :] = lines[pl.ds(1, most_h, stride=2), :].astype(BF)
         tail = [lines[pl.ds(2 * most_h + half, count - most_h, stride=2), :] for half in range(2)]
-        out[u, 2 * most_h :, :] = jnp.concatenate(tail, axis=0).astype(BF)
-        return carry
-
-    lax.fori_loop(0, out.shape[0], fetch, 0)
-
-
-def scatter_kernel(idx, grads, out, stage, *sums, most_h):
+        send[u, 2 * most_h :, :] = jnp.concatenate(tail, axis=0).astype(BF)
+        return carry
+
+    part = send.shape[0] // pieces
+    puts = []
+    for i in range(pieces):
+        lax.fori_loop(i * part, (i + 1) * part, fetch, 0)
+        at = pl.ds(i * part, part)
+        puts.append(pltpu.make_async_copy(send.at[at], out.at[at], out_sems.at[i]))
+        puts[i].start()
+    for put in puts:
+        put.wait()
+
+
+def scatter_kernel(idx, grads_in, out, grads, result, stage, in_sems, out_sems, *sums, most_h):
     count = stage.shape[0]
+    lanes = len(sums)
+    pieces = 4
     lines = stage.reshape(2 * count, 128)
+    part = grads.shape[0] // pieces
+    loads = []
+    for i in range(pieces):
+        at = pl.ds(i * part, part)
+        loads.append(pltpu.make_async_copy(grads_in.at[at], grads.at[at], in_sems.at[i]))
+        loads[i].start()
     for total in sums:
         total[...] = jnp.zeros_like(total)
 
@@ -96,15 +126,19 @@
         lines[pl.ds(1, most_h, stride=2), :] = block[most_h : 2 * most_h]
         lines[pl.ds(2 * most_h, count - most_h, stride=2), :] = block[2 * most_h : most_h + count]
         lines[pl.ds(2 * most_h + 1, count - most_h, stride=2), :] = block[most_h + count :]
-        for s in range(count):
-            total = sums[s % len(sums)]
-            at = idx[u, s]
-            total[at] = total[at] + stage[s]
-        return carry
-
-    lax.fori_loop(0, grads.shape[0], add, 0)
+        for first in range(0, count, lanes):
+            places = [idx[u, first + k] for k in range(lanes)]
+            values = [sums[k][places[k]] + stage[first + k] for k in range(lanes)]
+            for k in range(lanes):
+                sums[k][places[k]] = values[k]
+        return carry
+
+    for i in range(pieces):
+        loads[i].wait()
+        lax.fori_loop(i * part, (i + 1) * part, add, 0)
     chunk = 128
-    flats = [total.reshape(2 * out.shape[0], 128) for total in sums]
+    n_rows = result.shape[0]
+    flats = [total.reshape(2 * n_rows, 128) for total in sums]
 
     def finish(i, carry):
         at = pl.multiple_of(i * chunk, chunk)
@@ -113,10 +147,18 @@
             total = flats[0][from_rows, :]
             for flat in flats[1:]:
                 total = total + flat[from_rows, :]
-            out[pl.ds(at, chunk), half * 128 : half * 128 + 128] = total
-        return carry
-
-    lax.fori_loop(0, out.shape[0] // chunk, finish, 0)
+            result[pl.ds(at, chunk), half * 128 : half * 128 + 128] = total
+        return carry
+
+    part = n_rows // pieces
+    puts = []
+    for i in range(pieces):
+        lax.fori_loop(i * part // chunk, (i + 1) * part // chunk, finish, 0)
+        at = pl.ds(i * part, part)
+        puts.append(pltpu.make_async_copy(result.at[at], out.at[at], out_sems.at[i]))
+        puts[i].start()
+    for put in puts:
+        put.wait()
 
 
 def user_kernel(
@@ -288,10 +330,19 @@
     me = lax.axis_index("cols").astype(jnp.int32)
     V, S, A = VMEM_SPEC, SMEM_SPEC, pl.BlockSpec(memory_space=pl.ANY)
     req, h_pos, c_pos = call(
-        request_kernel, "requests", 16,
+        request_kernel, "requests", 62,
         (shape((n_rows, users, 128), jnp.int32), shape((1, hist), jnp.int32), shape((1, cand), jnp.int32)),
-        [S, V, V, V, V], (V, V, V), rows=n_rows, most_h=most_h, most_c=most_c,
-    )(me.reshape(1), history_owner[:, :, 0], history_row, candidate_owner[:, :, 0], candidate_row)
+        [S, A, A, A, A], (V, V, V),
+        [
+            pltpu.VMEM((users, 1, hist), jnp.int32), pltpu.VMEM((users, hist), jnp.int32),
+            pltpu.VMEM((users, 1, cand), jnp.int32), pltpu.VMEM((users, cand), jnp.int32),
+            pltpu.SemaphoreType.DMA((4,)),
+        ],
+        rows=n_rows, most_h=most_h, most_c=most_c,
+    )(
+        me.reshape(1), history_owner.transpose(0, 2, 1), history_row,
+        candidate_owner.transpose(0, 2, 1), candidate_row,
+    )
     wanted = lax.all_to_all(req, "rows", split_axis=0, concat_axis=0, tiled=True)
     wanted = wanted.reshape(peers, 128)
 
@@ -300,8 +351,13 @@
 
     count = most_h + most_c
     found = call(
-        gather_kernel, "gather_rows", 24, shape((peers, 2 * count, 128), BF), [S, V], V,
-        [pltpu.VMEM((table_rows, 2, 128), F32), pltpu.VMEM((count, 2, 128), F32)], most_h=most_h,
+        gather_kernel, "gather_rows", 62, shape((peers, 2 * count, 128), BF), [S, A], A,
+        [
+            pltpu.VMEM((table_rows, col_width), BF), pltpu.VMEM((table_rows, 2, 128), F32),
+            pltpu.VMEM((count, 2, 128), F32), pltpu.VMEM((peers, 2 * count, 128), BF),
+            pltpu.SemaphoreType.DMA((4,)), pltpu.SemaphoreType.DMA((4,)),
+        ],
+        most_h=most_h,
     )(wanted, embed_table)
     back = exchange(found)
     length = lax.dynamic_slice_in_dim(history_length, me, 1)
@@ -337,8 +393,14 @@
     )
     grads = exchange(send.reshape(peers, 2 * count, 128))
     table_grad = call(
-        scatter_kernel, "scatter_rows", 32, shape((table_rows, col_width), F32), [S, V], V,
-        [pltpu.VMEM((count, 2, 128), F32)] + [pltpu.VMEM((table_rows, 2, 128), F32)] * 2, most_h=most_h,
+        scatter_kernel, "scatter_rows", 62, shape((table_rows, col_width), F32), [S, A], A,
+        [
+            pltpu.VMEM((peers, 2 * count, 128), BF), pltpu.VMEM((table_rows, col_width), F32),
+            pltpu.VMEM((count, 2, 128), F32),
+            pltpu.SemaphoreType.DMA((4,)), pltpu.SemaphoreType.DMA((4,)),
+        ]
+        + [pltpu.VMEM((table_rows, 2, 128), F32)] * 4,
+        most_h=most_h,
     )(wanted, grads)
     return (logits, table_grad)
 

time: 267 us -> 257 us (0.963)
  local copies, waits for them, and re-layouts: 7.26 us -> 0.67 us
  Pallas kernels: 115 us -> 110 us
    unnamed x18 -> x4, local copies, waits for them, and re-layouts: 6.62 us -> 0.01 us
    pallas_call x3, Pallas kernels: 48.4 us -> 43.6 us  [the longest x1 23.5 us: body(): call(scatter_kernel, 'scatter_rows', 62, shape((table_rows, col_width), F...]
where the time goes in v2:
time: 257 us; the launch traced here: 256 us
  Pallas kernels  110 us (43%)
  blocking collectives  79.9 us (31%)
  waiting for transfers between devices  54 us (21%)
  starting transfers between devices  7.03 us (3%)
  matrix products  3.92 us (2%)
    pallas_call x1, Pallas kernels, body(): call(user_kernel, 'user_pass', 60, (shape((n_rows, n_cols, 2 * count, 128...  66.3 us
    all_to_all x1, blocking collectives, exchange(): lax.all_to_all(x, ('rows', 'cols'), split_axis=0, concat_axis=0, tiled=True)  63.8 us
    all_to_all x1, waiting for transfers between devices, exchange(): lax.all_to_all(x, ('rows', 'cols'), split_axis=0, concat_axis=0, tiled=True)  54 us
    pallas_call x1, Pallas kernels, body(): call(scatter_kernel, 'scatter_rows', 62, shape((table_rows, col_width), F...  23.5 us
    all_to_all x1, blocking collectives, body(): lax.all_to_all(req, 'rows', split_axis=0, concat_axis=0, tiled=True)  16.1 us
    pallas_call x1, Pallas kernels, body(): call(gather_kernel, 'gather_rows', 62, shape((peers, 2 * count, 128), BF)...  15.3 us
    all_to_all x1, starting transfers between devices, exchange(): lax.all_to_all(x, ('rows', 'cols'), split_axis=0, concat_axis=0, tiled=True)  7.03 us
  transfers between devices with their start and end apart: 1, of which 1 were waited for; matrix products, arithmetic and copies ran while one was open for 2% of the time, Pallas kernels for 0%

profile of v2, /device:TPU:1, one launch (start us, length us, event | category | flops | bytes accessed | tf_op | source)
XLA Modules:
  0.0 256.2 jit_solution(632884423328646849)
XLA Ops:
  0.6 4.8 %requests.1 = (s32[32,4,128]{2,1,0:T(4,128)}, s32[1,1024]{1,0:T(1,128)}, s32[1,512]{1,0:T(1,128)}) custom-call(s32[1]{0:T(128)} %bitcast.me, s32[4,1,1024]{2,1,0:T(1,128)} %bitcast.18, s32[4,1024]{1,0:T(4,128)} %h_row_in.1, s32[4,1,512]{2,1,0:T(1,128)} %bitcast.19, s32[4,512]{1,0:T(4,128)} %c_row_in.1), custom_call_target="tpu_custom_call" | custom-call | tf_op jit(solution)/shard_map/requests/pallas_call | solution.py:332
  5.4 16.1 %all_to_all.15 = s32[32,4,128]{2,1,0:T(4,128)} all-to-all(s32[32,4,128]{2,1,0:T(4,128)} %get-tuple-element.7), channel_id=1, replica_groups=mesh['rows'=32,'cols'=4] {'rows'}, dimensions={0} | all-to-all | bytes 131072 | tf_op jit(solution)/shard_map/all_to_all | solution.py:346
  21.5 15.3 %gather_rows.1 = bf16[128,144,128]{2,1,0:T(8,128)(2,1)} custom-call(s32[128,128]{1,0:T(8,128)} %bitcast.14, bf16[4096,256]{1,0:T(8,128)(2,1)} %table_in.1), custom_call_target="tpu_custom_call" | custom-call | tf_op jit(solution)/shard_map/gather_rows/pallas_call | solution.py:353
  36.8 0.0 copy-start.1
  36.8 0.0 copy-start
  36.8 7.0 %all-to-all-start.1 = ((bf16[128,144,128]{2,1,0:T(8,128)(2,1)}), bf16[128,144,128]{2,1,0:T(8,128)(2,1)}, u32[]{:S(2)}, u32[]{:S(2)}) async-start(bf16[128,144,128]{2,1,0:T(8,128)(2,1)} %gather_rows.1), calls=%async_computation.1 | async-start | bytes 9437184 | tf_op jit(solution)/shard_map/all_to_all | solution.py:350
  43.9 0.0 copy-done.1
  43.9 0.7 dynamic_slice.3.length
  44.5 0.0 copy-done
  44.5 3.9 %fusion.u_row = f32[1,1024]{1,0:T(1,128)} fusion(f32[1024,1]{0,1:T(1,128)S(1)} %bitcast.17, bf16[2,1024,1024]{2,1,0:T(8,128)(2,1)} %wo_in.1), kind=kOutput, calls=%fused_computation | convolution fusion | flops 12582912 | bytes 2105344 | tf_op jit(solution)/shard_map/dot_general | solution.py:364
  48.4 54.0 %all-to-all-done.1 = bf16[128,144,128]{2,1,0:T(8,128)(2,1)} async-done(((bf16[128,144,128]{2,1,0:T(8,128)(2,1)}), bf16[128,144,128]{2,1,0:T(8,128)(2,1)}, u32[]{:S(2)}, u32[]{:S(2)}) %all-to-all-start.1) | async-done | bytes 4718624 | tf_op jit(solution)/shard_map/all_to_all | solution.py:350
  102.4 66.3 %user_pass.1 = (bf16[32,4,144,128]{3,2,1,0:T(8,128)(2,1)}, f32[1,512]{1,0:T(1,128)}) custom-call(s32[1]{0:T(128)} %dynamic_slice.3.length, bf16[32,4,144,128]{3,2,1,0:T(8,128)(2,1)} %bitcast.4.recv_in, bf16[2,1024,1024]{2,1,0:T(8,128)(2,1)} %wq_in.1, bf16[2,1024,1024]{2,1,0:T(8,128)(2,1)} %wo_in.1, s32[1,1024]{1,0:T(1,128)} %get-tuple-element.8.h_pos, ...), custom_call_target="tpu_custom_call" | custom-call | tf_op jit(solution)/shard_map/user_pass/pallas_call | solution.py:367
  168.7 63.8 %all_to_all.16.grads_in = bf16[128,144,128]{2,1,0:T(8,128)(2,1)} all-to-all(bf16[128,144,128]{2,1,0:T(8,128)(2,1)} %bitcast.13), channel_id=1, replica_groups=mesh['rows'=32,'cols'=4] {'rows','cols'}, dimensions={0} | all-to-all | bytes 9437184 | tf_op jit(solution)/shard_map/all_to_all | solution.py:350
  232.5 23.5 %scatter_rows.1 = f32[4096,256]{1,0:T(8,128)} custom-call(s32[128,128]{1,0:T(8,128)} %bitcast.15, bf16[128,144,128]{2,1,0:T(8,128)(2,1)} %all_to_all.16.grads_in), custom_call_target="tpu_custom_call" | custom-call | tf_op jit(solution)/shard_map/scatter_rows/pallas_call | solution.py:395
Async XLA Ops:
  36.8 7.1 %copy-start.1 = (s32[4]{0:T(128)S(1)}, s32[4]{0:T(128)}, u32[]{:S(2)}) copy-start(s32[4]{0:T(128)} %param.14) | copy-start | bytes 52
  36.8 7.7 %copy-start = (f32[1024]{0:T(1024)S(1)}, f32[1024]{0:T(1024)}, u32[]{:S(2)}) copy-start(f32[1024]{0:T(1024)} %param.18) | copy-start | bytes 12292
  36.8 65.6 %all-to-all-start.1 = ((bf16[128,144,128]{2,1,0:T(8,128)(2,1)}), bf16[128,144,128]{2,1,0:T(8,128)(2,1)}, u32[]{:S(2)}, u32[]{:S(2)}) async-start(bf16[128,144,128]{2,1,0:T(8,128)(2,1)} %gather_rows.1), calls=%async_computation.1 | async-start | bytes 9437184 | tf_op jit(solution)/shard_map/all_to_all | solution.py:350

commit v3 on v2

--- a/solution.py
+++ b/solution.py
@@ -36,17 +36,21 @@
     before = (iota((hist, hist), 0) < iota((hist, hist), 1)).astype(BF)
     for load in loads:
         load.wait()
+    earlier = []
+    for own in (h_own, c_own):
+        n = own.shape[2]
+        match = jnp.concatenate([(iota((rows, n), 0) == own[u]).astype(F32) for u in range(users)], axis=0)
+        earlier.append((match, dot(match.astype(BF), before[:n, :n], NN)))
     for u in range(users):
         parts = []
-        for own, row, base, most, pos in (
-            (h_own, h_row, 0, most_h, h_pos),
-            (c_own, c_row, most_h, most_c, c_pos),
+        for (matches, counts), row, base, pos in (
+            (earlier[0], h_row, 0, h_pos),
+            (earlier[1], c_row, most_h, c_pos),
         ):
             n = row.shape[1]
-            owner = own[u]
-            match = (iota((rows, n), 0) == owner).astype(F32)
-            earlier = dot(match.astype(BF), before[:n, :n], NN)
-            rank = jnp.sum(match * earlier, axis=0, keepdims=True).astype(jnp.int32)
+            owner = (h_own if pos is h_pos else c_own)[u]
+            match = matches[u * rows : (u + 1) * rows]
+            rank = jnp.sum(match * counts[u * rows : (u + 1) * rows], axis=0, keepdims=True).astype(jnp.int32)
 
             @pl.when(me[0] == u)
             def _():
@@ -189,16 +193,16 @@
         return recv[c, :, part[0] : part[1], :].reshape(slots, 128)
 
     hist_even, hist_odd, cands = (0, 48), (48, 96), (96, 144)
+    for load in loads[:cols]:
+        load.wait()
+    got = dot(pt_c[...], jnp.concatenate([slab(c, cands) for c in range(cols)], axis=1), TN).astype(BF)
     for c in range(cols):
-        loads[c].wait()
-        both = jnp.concatenate([slab(c, hist_even), slab(c, hist_odd)], axis=1)
-        keys[:, c * 256 : c * 256 + 256] = dot(pt_h[...], both, TN).astype(BF)
-        if c % 2:
-            got = dot(pt_c[...], jnp.concatenate([slab(c - 1, cands), slab(c, cands)], axis=1), TN).astype(BF)
-            for k in range(2):
-                at = (c - 1 + k) * 256
-                cand[:, at : at + 128] = got[:n_cand, k * 128 : k * 128 + 128]
-                cand[:, at + 128 : at + 256] = got[n_cand:, k * 128 : k * 128 + 128]
+        at = c * 256
+        cand[:, at : at + 128] = got[:n_cand, c * 128 : c * 128 + 128]
+        cand[:, at + 128 : at + 256] = got[n_cand:, c * 128 : c * 128 + 128]
+    for c in range(0, cols, 2):
+        slabs = [slab(c + k, part) for k in range(2) for part in (hist_even, hist_odd)]
+        keys[:, c * 256 : c * 256 + 512] = dot(pt_h[...], jnp.concatenate(slabs, axis=1), TN).astype(BF)
     for load in loads[cols:]:
         load.wait()
     q1[...] = dot(cand[...], wq[0], NN).astype(BF)

time: 257 us -> 254 us (0.988)
  no operation moved by 1% of the time
where the time goes in v3:
time: 254 us
  Pallas kernels  108 us (43%)
  blocking collectives  79.9 us (31%)
  waiting for transfers between devices  54 us (21%)
  starting transfers between devices  7.04 us (3%)
  matrix products  3.92 us (2%)
    pallas_call x1, Pallas kernels, body(): call(user_kernel, 'user_pass', 60, (shape((n_rows, n_cols, 2 * count, 128...  64.8 us
    all_to_all x1, blocking collectives, exchange(): lax.all_to_all(x, ('rows', 'cols'), split_axis=0, concat_axis=0, tiled=True)  63.8 us
    all_to_all x1, waiting for transfers between devices, exchange(): lax.all_to_all(x, ('rows', 'cols'), split_axis=0, concat_axis=0, tiled=True)  54 us
    pallas_call x1, Pallas kernels, body(): call(scatter_kernel, 'scatter_rows', 62, shape((table_rows, col_width), F...  24.1 us
    all_to_all x1, blocking collectives, body(): lax.all_to_all(req, 'rows', split_axis=0, concat_axis=0, tiled=True)  16.1 us
    pallas_call x1, Pallas kernels, body(): call(gather_kernel, 'gather_rows', 62, shape((peers, 2 * count, 128), BF)...  15.3 us
    all_to_all x1, starting transfers between devices, exchange(): lax.all_to_all(x, ('rows', 'cols'), split_axis=0, concat_axis=0, tiled=True)  7.04 us
  transfers between devices with their start and end apart: 1, of which 1 were waited for; matrix products, arithmetic and copies ran while one was open for 2% of the time, Pallas kernels for 0%

profile of v3, /device:TPU:1, one launch (start us, length us, event | category | flops | bytes accessed | tf_op | source)
XLA Modules:
  0.0 254.3 jit_solution(1908718992939917478)
XLA Ops:
  0.6 3.7 %requests.1 = (s32[32,4,128]{2,1,0:T(4,128)}, s32[1,1024]{1,0:T(1,128)}, s32[1,512]{1,0:T(1,128)}) custom-call(s32[1]{0:T(128)} %bitcast.me, s32[4,1,1024]{2,1,0:T(1,128)} %bitcast.18, s32[4,1024]{1,0:T(4,128)} %h_row_in.1, s32[4,1,512]{2,1,0:T(1,128)} %bitcast.19, s32[4,512]{1,0:T(4,128)} %c_row_in.1), custom_call_target="tpu_custom_call" | custom-call | tf_op jit(solution)/shard_map/requests/pallas_call | solution.py:336
  4.4 16.1 %all_to_all.15 = s32[32,4,128]{2,1,0:T(4,128)} all-to-all(s32[32,4,128]{2,1,0:T(4,128)} %get-tuple-element.7), channel_id=1, replica_groups=mesh['rows'=32,'cols'=4] {'rows'}, dimensions={0} | all-to-all | bytes 131072 | tf_op jit(solution)/shard_map/all_to_all | solution.py:350
  20.4 15.3 %gather_rows.1 = bf16[128,144,128]{2,1,0:T(8,128)(2,1)} custom-call(s32[128,128]{1,0:T(8,128)} %bitcast.14, bf16[4096,256]{1,0:T(8,128)(2,1)} %table_in.1), custom_call_target="tpu_custom_call" | custom-call | tf_op jit(solution)/shard_map/gather_rows/pallas_call | solution.py:357
  35.7 0.0 copy-start.1
  35.7 0.0 copy-start
  35.7 7.0 %all-to-all-start.1 = ((bf16[128,144,128]{2,1,0:T(8,128)(2,1)}), bf16[128,144,128]{2,1,0:T(8,128)(2,1)}, u32[]{:S(2)}, u32[]{:S(2)}) async-start(bf16[128,144,128]{2,1,0:T(8,128)(2,1)} %gather_rows.1), calls=%async_computation.1 | async-start | bytes 9437184 | tf_op jit(solution)/shard_map/all_to_all | solution.py:354
  42.8 0.0 copy-done.1
  42.8 0.7 dynamic_slice.3.length
  43.4 0.0 copy-done
  43.4 3.9 %fusion.u_row = f32[1,1024]{1,0:T(1,128)} fusion(f32[1024,1]{0,1:T(1,128)S(1)} %bitcast.17, bf16[2,1024,1024]{2,1,0:T(8,128)(2,1)} %wo_in.1), kind=kOutput, calls=%fused_computation | convolution fusion | flops 12582912 | bytes 2105344 | tf_op jit(solution)/shard_map/dot_general | solution.py:368
  47.4 54.0 %all-to-all-done.1 = bf16[128,144,128]{2,1,0:T(8,128)(2,1)} async-done(((bf16[128,144,128]{2,1,0:T(8,128)(2,1)}), bf16[128,144,128]{2,1,0:T(8,128)(2,1)}, u32[]{:S(2)}, u32[]{:S(2)}) %all-to-all-start.1) | async-done | bytes 4718624 | tf_op jit(solution)/shard_map/all_to_all | solution.py:354
  101.3 64.8 %user_pass.1 = (bf16[32,4,144,128]{3,2,1,0:T(8,128)(2,1)}, f32[1,512]{1,0:T(1,128)}) custom-call(s32[1]{0:T(128)} %dynamic_slice.3.length, bf16[32,4,144,128]{3,2,1,0:T(8,128)(2,1)} %bitcast.4.recv_in, bf16[2,1024,1024]{2,1,0:T(8,128)(2,1)} %wq_in.1, bf16[2,1024,1024]{2,1,0:T(8,128)(2,1)} %wo_in.1, s32[1,1024]{1,0:T(1,128)} %get-tuple-element.8.h_pos, ...), custom_call_target="tpu_custom_call" | custom-call | tf_op jit(solution)/shard_map/user_pass/pallas_call | solution.py:371
  166.2 63.8 %all_to_all.16.grads_in = bf16[128,144,128]{2,1,0:T(8,128)(2,1)} all-to-all(bf16[128,144,128]{2,1,0:T(8,128)(2,1)} %bitcast.13), channel_id=1, replica_groups=mesh['rows'=32,'cols'=4] {'rows','cols'}, dimensions={0} | all-to-all | bytes 9437184 | tf_op jit(solution)/shard_map/all_to_all | solution.py:354
  230.0 24.1 %scatter_rows.1 = f32[4096,256]{1,0:T(8,128)} custom-call(s32[128,128]{1,0:T(8,128)} %bitcast.15, bf16[128,144,128]{2,1,0:T(8,128)(2,1)} %all_to_all.16.grads_in), custom_call_target="tpu_custom_call" | custom-call | tf_op jit(solution)/shard_map/scatter_rows/pallas_call | solution.py:399
Async XLA Ops:
  35.7 7.1 %copy-start.1 = (s32[4]{0:T(128)S(1)}, s32[4]{0:T(128)}, u32[]{:S(2)}) copy-start(s32[4]{0:T(128)} %param.14) | copy-start | bytes 52
  35.7 7.7 %copy-start = (f32[1024]{0:T(1024)S(1)}, f32[1024]{0:T(1024)}, u32[]{:S(2)}) copy-start(f32[1024]{0:T(1024)} %param.18) | copy-start | bytes 12292
  35.7 65.6 %all-to-all-start.1 = ((bf16[128,144,128]{2,1,0:T(8,128)(2,1)}), bf16[128,144,128]{2,1,0:T(8,128)(2,1)}, u32[]{:S(2)}, u32[]{:S(2)}) async-start(bf16[128,144,128]{2,1,0:T(8,128)(2,1)} %gather_rows.1), calls=%async_computation.1 | async-start | bytes 9437184 | tf_op jit(solution)/shard_map/all_to_all | solution.py:354
